TPU v7x, 32 devices: a whole 2x2x4 slice. The times are simulated.
32 devices in a mesh: rows: 4 (over y, core), cols: 8 (over z, x).
Axes of the slice: x: 2, y: 2, z: 4, core: 2. Of those that a mesh axis runs over, the one named last changes fastest.
Arguments:
- prior: float32 [64, 512, 512], P('rows', 'cols'), may hold values from -6 to 6
- obs_cell: int32 [8, 128], replicated, may hold values from 0 to 32767, as said below
- obs_weight: float32 [8, 128, 8], replicated, may hold values from 0.1 to 1
- obs_value: float32 [8, 128], replicated, may hold values from -8 to 8
- obs_var: float32 [8, 128], replicated, may hold values from 0.25 to 4
- loc_mask: int32 [8, 32], replicated, may hold values from 0 to 1, as said below
- batch_order: int32 [8], replicated, may hold values from 0 to 7, each once
- kernel: float32 [8, 7, 7], replicated, may hold values from 0.005 to 0.04
- mixing: float32 [8, 8], replicated, may hold values from -2 to 2
Outputs:
- forecast: float32 [64, 512, 512], P('rows', 'cols')
Inputs may be any that keep to these rules, and one draw needn't show every extreme that they name: `obs_cell`: all 128 cells of one batch lie in one tile, rows r * 16 to (r + 1) * 16 - 1 and columns c * 64 to (c + 1) * 64 - 1, whose index is r * 8 + c. `loc_mask`: for each batch the tiles marked 1 form a rectangle of tiles that contains the tile of that batch's cells. `batch_order`: each batch appears once.
All inputs are finite; a program needn't handle non-finite values.
Results may differ from a plain program's by a relative error of at most 0.0003.
Values sent between devices are 32-bit elements; how exact they have to be, the bound alone decides.
No kernel may reach another device: no remote copies, remote signals or barrier semaphores. Data moves between devices by JAX's collectives and lax.ppermute only.
A program may use at most 128 MiB of HBM per device.

v0:
```python
import jax
import jax.numpy as jnp
from jax import lax
from jax.sharding import PartitionSpec as P

BATCHES = 8
KW = 7
HALFW = 48


def with_halo(shard, sides, width):
    for axis, dim in sides:
        size, length = (lax.axis_size(axis), shard.shape[dim])
        up = [(i, (i + 1) % size) for i in range(size - 1)]
        down = [(j, i) for i, j in up]
        last = lax.slice_in_dim(shard, length - width, length, axis=dim)
        initial = lax.slice_in_dim(shard, 0, width, axis=dim)
        before = lax.ppermute(last, axis, up)
        after = lax.ppermute(initial, axis, down)
        shard = jnp.concatenate([before, shard, after], axis=dim)
    return shard


def taper_weights(ratio):
    clamped = jnp.maximum(ratio, 1.0)
    inner_part = (((-0.25 * ratio + 0.5) * ratio + 0.625) * ratio - 5.0 / 3.0) * ratio * ratio + 1.0
    outer_part = (
        ((((ratio / 12.0 - 0.5) * ratio + 0.625) * ratio + 5.0 / 3.0) * ratio - 5.0) * ratio
        + 4.0
        - 2.0 / (3.0 * clamped)
    )
    return jnp.where(ratio <= 1.0, inner_part, jnp.where(ratio < 2.0, outer_part, 0.0))


def batch_gain(predicted, value_row, var_row):
    mean_pred = jnp.mean(predicted, axis=1)
    spread = predicted - mean_pred[:, None]
    variance = jnp.sum(spread * spread, axis=1) / (predicted.shape[1] - 1)
    denominator = variance + var_row
    shrink = 1.0 / (1.0 + jnp.sqrt(var_row / denominator))
    kalman_gain = ((value_row - mean_pred)[:, None] - shrink[:, None] * spread) / denominator[
        :, None
    ]
    return (spread, kalman_gain)


def refresh_block(block, first_row, first_col, cell_row, cell_col, spread, kalman_gain, active):
    rows_count, cols_count, channels = block.shape
    members = spread.shape[1]
    species = channels // members
    row_pos = (first_row + jnp.arange(rows_count, dtype=jnp.int32)).astype(jnp.float32)
    col_pos = (first_col + jnp.arange(cols_count, dtype=jnp.int32)).astype(jnp.float32)
    row_gap = row_pos[:, None, None] - cell_row.astype(jnp.float32)[None, None, :]
    col_gap = col_pos[None, :, None] - cell_col.astype(jnp.float32)[None, None, :]
    squared = row_gap * row_gap + col_gap * col_gap
    taper = taper_weights(jnp.sqrt(squared) / HALFW) * active
    taper = taper.reshape(rows_count * cols_count, cell_row.shape[0])
    members_view = block.reshape(rows_count * cols_count, species, members)
    covariance = jnp.einsum(
        "psm,im->psi", members_view, spread, precision=lax.Precision.HIGHEST
    ) / (members - 1)
    increment = jnp.einsum(
        "psi,im->psm", covariance * taper[:, None, :], kalman_gain, precision=lax.Precision.HIGHEST
    )
    return (members_view + increment).reshape(rows_count, cols_count, channels)


def refresh_tile(ensemble, row_start, col_start, cell_row, cell_col, spread, kalman_gain, active):
    pieces = refresh_block(
        ensemble, row_start + 0, col_start, cell_row, cell_col, spread, kalman_gain, active
    )
    return pieces


def local_prediction(ensemble, cell_row, cell_col, weights_rows, row_start, col_start):
    tile_height, tile_width, channels = ensemble.shape
    species = weights_rows.shape[1]
    members = channels // species
    local_row = cell_row - row_start
    local_col = cell_col - col_start
    inside = (
        (local_row >= 0) & (local_row < tile_height) & (local_col >= 0) & (local_col < tile_width)
    )
    flat_index = jnp.clip(local_row, 0, tile_height - 1) * tile_width + jnp.clip(
        local_col, 0, tile_width - 1
    )
    picked = ensemble.reshape(tile_height * tile_width, species, members)[flat_index]
    predicted = jnp.einsum("is,ism->im", weights_rows, picked, precision=lax.Precision.HIGHEST)
    return jnp.where(inside[:, None], predicted, 0.0)


def shards(prior, obs_cell, obs_weight, obs_value, obs_var, loc_mask, batch_order, kernel, mixing):
    tile_height, tile_width, channels = prior.shape
    species = kernel.shape[0]
    members = channels // species
    cols_count = lax.axis_size("cols")
    grid_width = tile_width * cols_count
    row_start = lax.axis_index("rows") * tile_height
    col_start = lax.axis_index("cols") * tile_width
    my_tile = lax.axis_index("rows") * cols_count + lax.axis_index("cols")
    ensemble = prior
    for position in range(BATCHES):
        current = batch_order[position]
        obs_cells = obs_cell[current]
        cell_row = obs_cells // grid_width
        cell_col = obs_cells % grid_width
        partial_value = local_prediction(
            ensemble, cell_row, cell_col, obs_weight[current], row_start, col_start
        )
        predicted = lax.psum(partial_value, ("rows", "cols"))
        spread, kalman_gain = batch_gain(predicted, obs_value[current], obs_var[current])
        active = loc_mask[current, my_tile].astype(jnp.float32)
        ensemble = refresh_tile(
            ensemble, row_start, col_start, cell_row, cell_col, spread, kalman_gain, active
        )
    halo_width = KW // 2
    padded = with_halo(ensemble, (("rows", 0), ("cols", 1)), 3)
    padded_width = tile_width + 2 * halo_width
    offsets = (
        jnp.arange(padded_width, dtype=jnp.int32)[None, :]
        - jnp.arange(tile_width, dtype=jnp.int32)[:, None]
    )
    onehot = (offsets[:, :, None] == jnp.arange(KW, dtype=jnp.int32)[None, None, :]).astype(
        jnp.float32
    )
    band_matrix = jnp.einsum("tak,xik->taxi", kernel, onehot, precision=lax.Precision.HIGHEST)
    padded_grid = padded.reshape(tile_height + 2 * halo_width, padded_width, species, members)
    smoothed = jnp.zeros((tile_height, tile_width, species, members), jnp.float32)
    for vertical in range(KW):
        smoothed = smoothed + jnp.einsum(
            "txi,yitm->yxtm",
            band_matrix[:, vertical],
            padded_grid[vertical : vertical + tile_height],
            precision=lax.Precision.HIGHEST,
        )
    mixed_field = jnp.einsum("st,yxtm->yxsm", mixing, smoothed, precision=lax.Precision.HIGHEST)
    return mixed_field.reshape(tile_height, tile_width, channels)


def solution(mesh):
    return jax.shard_map(
        shards,
        mesh=mesh,
        in_specs=(P("rows", "cols", None), P(), P(), P(), P(), P(), P(), P(), P()),
        out_specs=P("rows", "cols", None),
        check_vma=False,
    )
```

profile of v0, /device:TPU:1, one launch (start us, length us, event | category | flops | bytes accessed | tf_op | source)
XLA Modules:
  0.0 676.1 jit_solution(12245388337613379013)
XLA Ops:
  34.7 40.8 %psum.56 = f32[128,64]{0,1:T(8,128)S(1)} all-reduce(f32[128,64]{0,1:T(8,128)S(1)} %broadcast_select_fusion.7), channel_id=1, replica_groups=mesh['rows'=4,'cols'=8] {'rows','cols'}, use_global_device_ids=true, to_apply=%region_0.1 | all-reduce | flops 8192 | bytes 65536 | tf_op jit(solution)/shard_map/psum | solution.py:110
  91.1 40.8 %psum.57 = f32[128,64]{0,1:T(8,128)S(1)} all-reduce(f32[128,64]{0,1:T(8,128)S(1)} %broadcast_select_fusion.6), channel_id=1, replica_groups=mesh['rows'=4,'cols'=8] {'rows','cols'}, use_global_device_ids=true, to_apply=%region_3.4 | all-reduce | flops 8192 | bytes 65536 | tf_op jit(solution)/shard_map/psum | solution.py:110
  131.9 6.8 %fusion.242 = f32[1024,8,128]{2,0,1:T(8,128)S(1)} fusion(f32[1024,8,64]{0,2,1:T(8,128)S(1)} %fusion.60, f32[128,64]{0,1:T(8,128)S(1)} %psum.57, f32[128]{0:T(128)S(1)} %get-tuple-element.169), kind=kOutput, calls=%fused_computation.329 | convolution fusion | flops 805314560 | bytes 6324736 | tf_op jit(solution)/shard_map/psm,im->psi/dot_general | solution.py:59
  153.8 40.1 %psum.58 = f32[128,64]{0,1:T(8,128)S(1)} all-reduce(f32[128,64]{0,1:T(8,128)S(1)} %broadcast_select_fusion.5), channel_id=1, replica_groups=mesh['rows'=4,'cols'=8] {'rows','cols'}, use_global_device_ids=true, to_apply=%region_6.7 | all-reduce | flops 8192 | bytes 65536 | tf_op jit(solution)/shard_map/psum | solution.py:110
  194.1 6.8 %fusion.239 = f32[1024,8,128]{2,0,1:T(8,128)S(1)} fusion(f32[1024,8,64]{0,2,1:T(8,128)S(1)} %copy-done.2, f32[128,64]{0,1:T(8,128)S(1)} %psum.58, f32[128]{0:T(128)S(1)} %get-tuple-element.167), kind=kOutput, calls=%fused_computation.326 | convolution fusion | flops 805314560 | bytes 6324736 | tf_op jit(solution)/shard_map/psm,im->psi/dot_general | solution.py:59
  216.3 40.2 %psum.59 = f32[128,64]{0,1:T(8,128)S(1)} all-reduce(f32[128,64]{0,1:T(8,128)S(1)} %broadcast_select_fusion.4), channel_id=1, replica_groups=mesh['rows'=4,'cols'=8] {'rows','cols'}, use_global_device_ids=true, to_apply=%region_9.10 | all-reduce | flops 8192 | bytes 65536 | tf_op jit(solution)/shard_map/psum | solution.py:110
  256.6 6.8 %fusion.236 = f32[1024,8,128]{2,0,1:T(8,128)S(1)} fusion(f32[1024,8,64]{0,2,1:T(8,128)S(1)} %copy-done.3, f32[128,64]{0,1:T(8,128)S(1)} %psum.59, f32[128]{0:T(128)S(1)} %get-tuple-element.165), kind=kOutput, calls=%fused_computation.323 | convolution fusion | flops 805314560 | bytes 6324736 | tf_op jit(solution)/shard_map/psm,im->psi/dot_general | solution.py:59
  278.6 40.1 %psum.60 = f32[128,64]{0,1:T(8,128)S(1)} all-reduce(f32[128,64]{0,1:T(8,128)S(1)} %broadcast_select_fusion.3), channel_id=1, replica_groups=mesh['rows'=4,'cols'=8] {'rows','cols'}, use_global_device_ids=true, to_apply=%region_12.13 | all-reduce | flops 8192 | bytes 65536 | tf_op jit(solution)/shard_map/psum | solution.py:110
  318.8 6.8 %fusion.233 = f32[1024,8,128]{2,0,1:T(8,128)S(1)} fusion(f32[1024,8,64]{0,2,1:T(8,128)S(1)} %copy-done.4, f32[128,64]{0,1:T(8,128)S(1)} %psum.60, f32[128]{0:T(128)S(1)} %get-tuple-element.163), kind=kOutput, calls=%fused_computation.320 | convolution fusion | flops 805314560 | bytes 6324736 | tf_op jit(solution)/shard_map/psm,im->psi/dot_general | solution.py:59
  327.0 6.3 fusion.48
  341.0 40.2 %psum.61 = f32[128,64]{0,1:T(8,128)S(1)} all-reduce(f32[128,64]{0,1:T(8,128)S(1)} %broadcast_select_fusion.2), channel_id=1, replica_groups=mesh['rows'=4,'cols'=8] {'rows','cols'}, use_global_device_ids=true, to_apply=%region_15.16 | all-reduce | flops 8192 | bytes 65536 | tf_op jit(solution)/shard_map/psum | solution.py:110
  381.4 6.8 %fusion.230 = f32[1024,8,128]{2,0,1:T(8,128)S(1)} fusion(f32[1024,8,64]{0,2,1:T(8,128)S(1)} %copy-done.5, f32[128,64]{0,1:T(8,128)S(1)} %psum.61, f32[128]{0:T(128)S(1)} %get-tuple-element.161), kind=kOutput, calls=%fused_computation.317 | convolution fusion | flops 805314560 | bytes 6324736 | tf_op jit(solution)/shard_map/psm,im->psi/dot_general | solution.py:59
  403.2 40.3 %psum.62 = f32[128,64]{0,1:T(8,128)S(1)} all-reduce(f32[128,64]{0,1:T(8,128)S(1)} %broadcast_select_fusion.1), channel_id=1, replica_groups=mesh['rows'=4,'cols'=8] {'rows','cols'}, use_global_device_ids=true, to_apply=%region_18.19 | all-reduce | flops 8192 | bytes 65536 | tf_op jit(solution)/shard_map/psum | solution.py:110
  443.5 6.8 %fusion.227 = f32[1024,8,128]{2,0,1:T(8,128)S(1)} fusion(f32[1024,8,64]{0,2,1:T(8,128)S(1)} %copy-done.6, f32[128,64]{0,1:T(8,128)S(1)} %psum.62, f32[128]{0:T(128)S(1)} %get-tuple-element.159), kind=kOutput, calls=%fused_computation.314 | convolution fusion | flops 805314560 | bytes 6324736 | tf_op jit(solution)/shard_map/psm,im->psi/dot_general | solution.py:59
  462.7 40.7 %psum.63 = f32[128,64]{0,1:T(8,128)S(1)} all-reduce(f32[128,64]{0,1:T(8,128)S(1)} %broadcast_select_fusion), channel_id=1, replica_groups=mesh['rows'=4,'cols'=8] {'rows','cols'}, use_global_device_ids=true, to_apply=%region_21.22 | all-reduce | flops 8192 | bytes 65536 | tf_op jit(solution)/shard_map/psum | solution.py:110
  503.5 6.8 %fusion.224 = f32[1024,8,128]{2,0,1:T(8,128)S(1)} fusion(f32[1024,8,64]{0,2,1:T(8,128)S(1)} %fusion.54, f32[128,64]{0,1:T(8,128)S(1)} %psum.63, f32[128]{0:T(128)S(1)} %get-tuple-element.133), kind=kOutput, calls=%fused_computation.311 | convolution fusion | flops 805314560 | bytes 6324736 | tf_op jit(solution)/shard_map/psm,im->psi/dot_general | solution.py:59
  583.9 10.3 %fusion.10 = f32[8,16,64,64]{3,2,1,0:T(8,128)S(1)} fusion(f32[16,70,8,64]{3,2,1,0:T(8,128)} %reshape.2901, f32[8,64,70,1]{2,0,1,3:T(8,128)} %get-tuple-element.61), kind=kOutput, calls=%fused_computation.18 | convolution fusion | flops 440401920 | bytes 4534272 | tf_op jit(solution)/shard_map/txi,yitm->yxtm/dot_general | solution.py:130
  594.2 11.8 %fusion.12 = f32[8,16,64,64]{3,2,1,0:T(8,128)} fusion(f32[16,70,8,64]{3,2,1,0:T(8,128)} %reshape.2900, f32[8,64,70,1]{2,0,1,3:T(8,128)S(1)} %copy-done.17), kind=kOutput, calls=%fused_computation.20 | convolution fusion | flops 440401920 | bytes 4534272 | tf_op jit(solution)/shard_map/txi,yitm->yxtm/dot_general | solution.py:130
  606.1 9.4 %fusion.2 = f32[8,16,64,64]{3,2,1,0:T(8,128)} fusion(f32[16,70,8,64]{3,2,1,0:T(8,128)S(1)} %bitcast.856, f32[8,64,70,1]{2,0,1,3:T(8,128)S(1)} %copy-done.16), kind=kOutput, calls=%fused_computation.10 | convolution fusion | flops 440401920 | bytes 4534272 | tf_op jit(solution)/shard_map/txi,yitm->yxtm/dot_general | solution.py:130
  615.5 9.9 %fusion.4 = f32[8,16,64,64]{3,2,1,0:T(8,128)} fusion(f32[16,70,8,64]{3,2,1,0:T(8,128)S(1)} %bitcast.854, f32[8,64,70,1]{2,0,1,3:T(8,128)S(1)} %copy-done.15), kind=kOutput, calls=%fused_computation.12 | convolution fusion | flops 440401920 | bytes 4534272 | tf_op jit(solution)/shard_map/txi,yitm->yxtm/dot_general | solution.py:130
  625.4 9.5 %fusion.6 = f32[8,16,64,64]{3,2,1,0:T(8,128)} fusion(f32[16,70,8,64]{3,2,1,0:T(8,128)S(1)} %bitcast.852, f32[8,64,70,1]{2,0,1,3:T(8,128)S(1)} %copy-done.14), kind=kOutput, calls=%fused_computation.14 | convolution fusion | flops 440401920 | bytes 4534272 | tf_op jit(solution)/shard_map/txi,yitm->yxtm/dot_general | solution.py:130
  635.0 9.4 %fusion.8 = f32[8,16,64,64]{3,2,1,0:T(8,128)} fusion(f32[16,70,8,64]{3,2,1,0:T(8,128)S(1)} %bitcast.850, f32[8,64,70,1]{2,0,1,3:T(8,128)S(1)} %get-tuple-element.60), kind=kOutput, calls=%fused_computation.16 | convolution fusion | flops 440401920 | bytes 4534272 | tf_op jit(solution)/shard_map/txi,yitm->yxtm/dot_general | solution.py:130
  644.4 13.5 %add_bitcast_fusion = f32[16,64,8,64]{1,3,0,2:T(8,128)} fusion(f32[8,16,64,64]{3,2,1,0:T(8,128)S(1)} %copy-done.10, f32[8,16,64,64]{3,2,1,0:T(8,128)} %fusion.4, f32[8,16,64,64]{3,2,1,0:T(8,128)} %fusion.6, f32[8,16,64,64]{3,2,1,0:T(8,128)} %fusion.8, f32[8,16,64,64]{3,2,1,0:T(8,128)S(1)} %copy-done.9, f32[8,16,64,64]{3,2,1,0:T(8,128)S(1)} %fusion.10, ...), kind=kOutput, calls=%fused_computation.24 | convolution fusion | flops 443547648 | bytes 17117184 | tf_op jit(solution)/shard_map/txi,yitm->yxtm/dot_general | solution.py:130
  663.3 7.8 %convolution_bitcast_fusion = f32[16,64,8,64]{3,2,1,0:T(8,128)} fusion(f32[16,64,8,64]{3,2,1,0:T(8,128)} %copy.99, f32[8,8]{1,0:T(8,128)S(1)} %copy-done.45), kind=kOutput, calls=%fused_computation.40 | convolution fusion | flops 50331648 | bytes 4194560 | tf_op jit(solution)/shard_map/st,yxtm->yxsm/dot_general | solution.py:136
  (314 shorter events, 195.7 us)
Async XLA Ops:
  0.0 534.7 %copy-start = (f32[8,7,7]{2,0,1:T(8,128)S(1)}, f32[8,7,7]{2,0,1:T(8,128)}, u32[]{:S(2)}) copy-start(f32[8,7,7]{2,0,1:T(8,128)} %param.16) | copy-start | bytes 4708
  0.0 24.1 %copy-start.13 = (f32[16,64,512]{2,1,0:T(8,128)S(1)}, f32[16,64,512]{2,1,0:T(8,128)}, u32[]{:S(2)}) copy-start(f32[16,64,512]{2,1,0:T(8,128)} %param.9) | copy-start | bytes 6291460
  29.4 50.4 %copy-start.8 = (f32[1024,8,64]{0,2,1:T(8,128)}, f32[1024,8,64]{0,2,1:T(8,128)S(1)}, u32[]{:S(2)}) copy-start(f32[1024,8,64]{0,2,1:T(8,128)S(1)} %copy.67) | copy-start | bytes 6291460
  85.0 46.9 %copy-start.46 = (f32[8,128]{1,0:T(8,128)S(1)}, f32[8,128]{1,0:T(8,128)}, u32[]{:S(2)}) copy-start(f32[8,128]{1,0:T(8,128)} %param.12) | copy-start | bytes 12292
  87.7 51.0 %copy-start.47 = (f32[8,128]{1,0:T(8,128)S(1)}, f32[8,128]{1,0:T(8,128)}, u32[]{:S(2)}) copy-start(f32[8,128]{1,0:T(8,128)} %param.13) | copy-start | bytes 12292
  87.8 51.6 %copy-start.22 = (f32[16,128]{1,0:T(8,128)S(1)}, f32[16,128]{1,0:T(8,128)}, u32[]{:S(2)}) copy-start(f32[16,128]{1,0:T(8,128)} %get-tuple-element.135) | copy-start | bytes 24580
  146.4 47.7 %copy-start.2 = (f32[1024,8,64]{0,2,1:T(8,128)S(1)}, f32[1024,8,64]{0,2,1:T(8,128)}, u32[]{:S(2)}) copy-start(f32[1024,8,64]{0,2,1:T(8,128)} %fusion.39) | copy-start | bytes 6291460
  150.5 51.0 %copy-start.21 = (f32[16,128]{1,0:T(8,128)S(1)}, f32[16,128]{1,0:T(8,128)}, u32[]{:S(2)}) copy-start(f32[16,128]{1,0:T(8,128)} %get-tuple-element.136) | copy-start | bytes 24580
  208.6 48.0 %copy-start.3 = (f32[1024,8,64]{0,2,1:T(8,128)S(1)}, f32[1024,8,64]{0,2,1:T(8,128)}, u32[]{:S(2)}) copy-start(f32[1024,8,64]{0,2,1:T(8,128)} %fusion.42) | copy-start | bytes 6291460
  213.0 51.1 %copy-start.20 = (f32[16,128]{1,0:T(8,128)S(1)}, f32[16,128]{1,0:T(8,128)}, u32[]{:S(2)}) copy-start(f32[16,128]{1,0:T(8,128)} %get-tuple-element.137) | copy-start | bytes 24580
  271.1 47.7 %copy-start.4 = (f32[1024,8,64]{0,2,1:T(8,128)S(1)}, f32[1024,8,64]{0,2,1:T(8,128)}, u32[]{:S(2)}) copy-start(f32[1024,8,64]{0,2,1:T(8,128)} %fusion.45) | copy-start | bytes 6291460
  275.3 51.0 %copy-start.19 = (f32[16,128]{1,0:T(8,128)S(1)}, f32[16,128]{1,0:T(8,128)}, u32[]{:S(2)}) copy-start(f32[16,128]{1,0:T(8,128)} %get-tuple-element.138) | copy-start | bytes 24580
  333.3 48.0 %copy-start.5 = (f32[1024,8,64]{0,2,1:T(8,128)S(1)}, f32[1024,8,64]{0,2,1:T(8,128)}, u32[]{:S(2)}) copy-start(f32[1024,8,64]{0,2,1:T(8,128)} %fusion.48) | copy-start | bytes 6291460
  337.7 51.1 %copy-start.18 = (f32[16,128]{1,0:T(8,128)S(1)}, f32[16,128]{1,0:T(8,128)}, u32[]{:S(2)}) copy-start(f32[16,128]{1,0:T(8,128)} %get-tuple-element.139) | copy-start | bytes 24580
  395.8 47.6 %copy-start.6 = (f32[1024,8,64]{0,2,1:T(8,128)S(1)}, f32[1024,8,64]{0,2,1:T(8,128)}, u32[]{:S(2)}) copy-start(f32[1024,8,64]{0,2,1:T(8,128)} %fusion.51) | copy-start | bytes 6291460
  521.4 14.1 %collective-permute-start = (f32[3,64,512]{2,1,0:T(8,128)}, f32[3,64,512]{2,1,0:T(8,128)}, u32[]{:S(2)}, u32[]{:S(2)}) collective-permute-start(f32[3,64,512]{2,1,0:T(8,128)} %slice.114), channel_id=1, source_target_pairs={{0,8},{8,16},{16,24},{1,9},{9,17},{17,25},{2,10},{10,18},{18,26},{... | collective-permute-start | bytes 1179656 | tf_op jit(solution)/shard_map/ppermute | solution.py:18
  527.4 9.1 %collective-permute-start.1 = (f32[3,64,512]{2,1,0:T(8,128)S(1)}, f32[3,64,512]{2,1,0:T(8,128)S(1)}, u32[]{:S(2)}, u32[]{:S(2)}) collective-permute-start(f32[3,64,512]{2,1,0:T(8,128)S(1)} %slice.116), channel_id=1, source_target_pairs={{8,0},{16,8},{24,16},{9,1},{17,9},{25,17},{10,2},{18,10},{26,18},{... | collective-permute-start | bytes 1179656 | tf_op jit(solution)/shard_map/ppermute | solution.py:19
  537.4 9.4 %collective-permute-start.2 = (f32[22,3,512]{2,1,0:T(4,128)S(1)}, f32[22,3,512]{2,1,0:T(4,128)S(1)}, u32[]{:S(2)}, u32[]{:S(2)}) collective-permute-start(f32[22,3,512]{2,1,0:T(4,128)S(1)} %get-tuple-element.52), channel_id=1, source_target_pairs={{0,1},{1,2},{2,3},{3,4},{4,5},{5,6},{6,7},{8,9},{9,10},{10,11},{11... | collective-permute-start | bytes 405512 | tf_op jit(solution)/shard_map/ppermute | solution.py:18
  540.5 6.4 collective-permute-start.3
  581.3 24.8 %slice-start.6 = ((s8[4587520]{0:T(1024)(128)(4,1)}), s8[393216]{0:T(1024)(128)(4,1)S(1)}, s32[]{:S(2)}) async-start(s8[4587520]{0:T(1024)(128)(4,1)} %bitcast.855), calls=%async_computation.6 | async-start | bytes 786432
  583.9 22.2 %slice-start.7 = ((s8[4587520]{0:T(1024)(128)(4,1)}), s8[4194304]{0:T(1024)(128)(4,1)S(1)}, s32[]{:S(2)}) async-start(s8[4587520]{0:T(1024)(128)(4,1)} %bitcast.855), calls=%async_computation.7 | async-start | bytes 8388608
  594.2 21.3 %slice-start.4 = ((s8[4587520]{0:T(1024)(128)(4,1)}), s8[4194304]{0:T(1024)(128)(4,1)S(1)}, s32[]{:S(2)}) async-start(s8[4587520]{0:T(1024)(128)(4,1)} %bitcast.853), calls=%async_computation.4 | async-start | bytes 8388608
  594.2 31.2 %slice-start.2 = ((s8[4587520]{0:T(1024)(128)(4,1)}), s8[4194304]{0:T(1024)(128)(4,1)S(1)}, s32[]{:S(2)}) async-start(s8[4587520]{0:T(1024)(128)(4,1)} %bitcast.851), calls=%async_computation.2 | async-start | bytes 8388608
  615.5 19.4 %slice-start = ((s8[4587520]{0:T(1024)(128)(4,1)}), s8[4194304]{0:T(1024)(128)(4,1)S(1)}, s32[]{:S(2)}) async-start(s8[4587520]{0:T(1024)(128)(4,1)} %bitcast.849), calls=%async_computation | async-start | bytes 8388608
  (52 other events, 353.9 us)
where the time goes:
time: 687 us; the launch traced here: 676 us
  blocking collectives  323 us (47%)
  matrix products  179 us (26%)
  local copies, waits for them, and re-layouts  118 us (17%)
  between operations  21.8 us (3%)
  other arithmetic  17 us (2%)
  starting transfers between devices  11.7 us (2%)
    psum x8, blocking collectives, shards(): predicted = lax.psum(partial_value, ('rows', 'cols'))  323 us
    dot_general x7, matrix products, shards(): jnp.einsum('txi,yitm->yxtm', band_matrix[:, vertical], padded_grid[vertic...  73.8 us
    dot_general x8, matrix products, refresh_block(): jnp.einsum('psm,im->psi', members_view, spread, precision=lax.Precision.H...  50.9 us
    dot_general x8, matrix products, refresh_block(): jnp.einsum('psi,im->psm', covariance * taper[:, None, :], kalman_gain, pr...  45.7 us
    slice x8, local copies, waits for them, and re-layouts, shards(): padded_grid[vertical:vertical + tile_height]  35.5 us
    add x7, local copies, waits for them, and re-layouts, refresh_block(): return (members_view + increment).reshape(rows_count, cols_count, channels)  26.4 us
    gather x8, local copies, waits for them, and re-layouts, local_prediction(): ensemble.reshape(tile_height * tile_width, species, members)[flat_index]  23.4 us
  transfers between devices with their start and end apart: 4, of which 3 were waited for; matrix products, arithmetic and copies ran while one was open for 1% of the time, Pallas kernels for 0%

commit v1 on v0

--- a/solution.py
+++ b/solution.py
@@ -107,7 +107,7 @@
         partial_value = local_prediction(
             ensemble, cell_row, cell_col, obs_weight[current], row_start, col_start
         )
-        predicted = lax.psum(partial_value, ("rows", "cols"))
+        predicted = lax.psum(lax.psum(partial_value, "cols"), "rows")
         spread, kalman_gain = batch_gain(predicted, obs_value[current], obs_var[current])
         active = loc_mask[current, my_tile].astype(jnp.float32)
         ensemble = refresh_tile(

time: 687 us -> 712 us (1.036)
  blocking collectives: 323 us -> 352 us
    psum x8 -> x16, blocking collectives: 323 us -> 352 us  [shards(): predicted = lax.psum(lax.psum(partial_value, 'cols'), 'rows')]
where the time goes in v1:
time: 712 us; the launch traced here: 702 us
  blocking collectives  352 us (49%)
  matrix products  179 us (25%)
  local copies, waits for them, and re-layouts  119 us (17%)
  between operations  21.8 us (3%)
  other arithmetic  17 us (2%)
  starting transfers between devices  8.28 us (1%)
    psum x16, blocking collectives, shards(): predicted = lax.psum(lax.psum(partial_value, 'cols'), 'rows')  352 us
    dot_general x7, matrix products, shards(): jnp.einsum('txi,yitm->yxtm', band_matrix[:, vertical], padded_grid[vertic...  73.8 us
    dot_general x8, matrix products, refresh_block(): jnp.einsum('psm,im->psi', members_view, spread, precision=lax.Precision.H...  50.9 us
    dot_general x8, matrix products, refresh_block(): jnp.einsum('psi,im->psm', covariance * taper[:, None, :], kalman_gain, pr...  45.7 us
    slice x8, local copies, waits for them, and re-layouts, shards(): padded_grid[vertical:vertical + tile_height]  35.4 us
    add x7, local copies, waits for them, and re-layouts, refresh_block(): return (members_view + increment).reshape(rows_count, cols_count, channels)  27.1 us
    gather x8, local copies, waits for them, and re-layouts, local_prediction(): ensemble.reshape(tile_height * tile_width, species, members)[flat_index]  23.5 us
  transfers between devices with their start and end apart: 4, of which 3 were waited for; matrix products, arithmetic and copies ran while one was open for 1% of the time, Pallas kernels for 0%

profile of v1, /device:TPU:1, one launch (start us, length us, event | category | flops | bytes accessed | tf_op | source)
XLA Modules:
  0.0 702.3 jit_solution(4542431917750629813)
XLA Ops:
  34.9 31.1 %psum.112 = f32[128,64]{0,1:T(8,128)S(1)} all-reduce(f32[128,64]{0,1:T(8,128)S(1)} %broadcast_select_fusion.7), channel_id=1, replica_groups=mesh['rows'=4,'cols'=8] {'cols'}, use_global_device_ids=true, to_apply=%region_0.1 | all-reduce | flops 8192 | bytes 65536 | tf_op jit(solution)/shard_map/psum | solution.py:110
  66.0 17.7 %psum.113 = f32[128,64]{0,1:T(8,128)S(1)} all-reduce(f32[128,64]{0,1:T(8,128)S(1)} %psum.112), channel_id=1, replica_groups=mesh['rows'=4,'cols'=8] {'rows'}, use_global_device_ids=true, to_apply=%region_1.2 | all-reduce | flops 8192 | bytes 65536 | tf_op jit(solution)/shard_map/psum | solution.py:110
  99.2 26.1 %psum.114 = f32[128,64]{0,1:T(8,128)S(1)} all-reduce(f32[128,64]{0,1:T(8,128)S(1)} %broadcast_select_fusion.6), channel_id=1, replica_groups=mesh['rows'=4,'cols'=8] {'cols'}, use_global_device_ids=true, to_apply=%region_4.5 | all-reduce | flops 8192 | bytes 65536 | tf_op jit(solution)/shard_map/psum | solution.py:110
  125.3 17.4 %psum.115 = f32[128,64]{0,1:T(8,128)S(1)} all-reduce(f32[128,64]{0,1:T(8,128)S(1)} %psum.114), channel_id=1, replica_groups=mesh['rows'=4,'cols'=8] {'rows'}, use_global_device_ids=true, to_apply=%region_5.6 | all-reduce | flops 8192 | bytes 65536 | tf_op jit(solution)/shard_map/psum | solution.py:110
  165.0 26.1 %psum.116 = f32[128,64]{0,1:T(8,128)S(1)} all-reduce(f32[128,64]{0,1:T(8,128)S(1)} %broadcast_select_fusion.5), channel_id=1, replica_groups=mesh['rows'=4,'cols'=8] {'cols'}, use_global_device_ids=true, to_apply=%region_8.9 | all-reduce | flops 8192 | bytes 65536 | tf_op jit(solution)/shard_map/psum | solution.py:110
  191.1 17.2 %psum.117 = f32[128,64]{0,1:T(8,128)S(1)} all-reduce(f32[128,64]{0,1:T(8,128)S(1)} %psum.116), channel_id=1, replica_groups=mesh['rows'=4,'cols'=8] {'rows'}, use_global_device_ids=true, to_apply=%region_9.10 | all-reduce | flops 8192 | bytes 65536 | tf_op jit(solution)/shard_map/psum | solution.py:110
  230.2 26.1 %psum.118 = f32[128,64]{0,1:T(8,128)S(1)} all-reduce(f32[128,64]{0,1:T(8,128)S(1)} %broadcast_select_fusion.4), channel_id=1, replica_groups=mesh['rows'=4,'cols'=8] {'cols'}, use_global_device_ids=true, to_apply=%region_12.13 | all-reduce | flops 8192 | bytes 65536 | tf_op jit(solution)/shard_map/psum | solution.py:110
  256.3 17.2 %psum.119 = f32[128,64]{0,1:T(8,128)S(1)} all-reduce(f32[128,64]{0,1:T(8,128)S(1)} %psum.118), channel_id=1, replica_groups=mesh['rows'=4,'cols'=8] {'rows'}, use_global_device_ids=true, to_apply=%region_13.14 | all-reduce | flops 8192 | bytes 65536 | tf_op jit(solution)/shard_map/psum | solution.py:110
  295.9 26.1 %psum.120 = f32[128,64]{0,1:T(8,128)S(1)} all-reduce(f32[128,64]{0,1:T(8,128)S(1)} %broadcast_select_fusion.3), channel_id=1, replica_groups=mesh['rows'=4,'cols'=8] {'cols'}, use_global_device_ids=true, to_apply=%region_16.17 | all-reduce | flops 8192 | bytes 65536 | tf_op jit(solution)/shard_map/psum | solution.py:110
  322.0 17.2 %psum.121 = f32[128,64]{0,1:T(8,128)S(1)} all-reduce(f32[128,64]{0,1:T(8,128)S(1)} %psum.120), channel_id=1, replica_groups=mesh['rows'=4,'cols'=8] {'rows'}, use_global_device_ids=true, to_apply=%region_17.18 | all-reduce | flops 8192 | bytes 65536 | tf_op jit(solution)/shard_map/psum | solution.py:110
  361.2 26.1 %psum.122 = f32[128,64]{0,1:T(8,128)S(1)} all-reduce(f32[128,64]{0,1:T(8,128)S(1)} %broadcast_select_fusion.2), channel_id=1, replica_groups=mesh['rows'=4,'cols'=8] {'cols'}, use_global_device_ids=true, to_apply=%region_20.21 | all-reduce | flops 8192 | bytes 65536 | tf_op jit(solution)/shard_map/psum | solution.py:110
  387.3 17.2 %psum.123 = f32[128,64]{0,1:T(8,128)S(1)} all-reduce(f32[128,64]{0,1:T(8,128)S(1)} %psum.122), channel_id=1, replica_groups=mesh['rows'=4,'cols'=8] {'rows'}, use_global_device_ids=true, to_apply=%region_21.22 | all-reduce | flops 8192 | bytes 65536 | tf_op jit(solution)/shard_map/psum | solution.py:110
  426.7 26.1 %psum.124 = f32[128,64]{0,1:T(8,128)S(1)} all-reduce(f32[128,64]{0,1:T(8,128)S(1)} %broadcast_select_fusion.1), channel_id=1, replica_groups=mesh['rows'=4,'cols'=8] {'cols'}, use_global_device_ids=true, to_apply=%region_24.25 | all-reduce | flops 8192 | bytes 65536 | tf_op jit(solution)/shard_map/psum | solution.py:110
  452.8 17.2 %psum.125 = f32[128,64]{0,1:T(8,128)S(1)} all-reduce(f32[128,64]{0,1:T(8,128)S(1)} %psum.124), channel_id=1, replica_groups=mesh['rows'=4,'cols'=8] {'rows'}, use_global_device_ids=true, to_apply=%region_25.26 | all-reduce | flops 8192 | bytes 65536 | tf_op jit(solution)/shard_map/psum | solution.py:110
  489.5 26.1 %psum.126 = f32[128,64]{0,1:T(8,128)S(1)} all-reduce(f32[128,64]{0,1:T(8,128)S(1)} %broadcast_select_fusion), channel_id=1, replica_groups=mesh['rows'=4,'cols'=8] {'cols'}, use_global_device_ids=true, to_apply=%region_28.29 | all-reduce | flops 8192 | bytes 65536 | tf_op jit(solution)/shard_map/psum | solution.py:110
  515.6 17.2 %psum.127 = f32[128,64]{0,1:T(8,128)S(1)} all-reduce(f32[128,64]{0,1:T(8,128)S(1)} %psum.126), channel_id=1, replica_groups=mesh['rows'=4,'cols'=8] {'rows'}, use_global_device_ids=true, to_apply=%region_29.30 | all-reduce | flops 8192 | bytes 65536 | tf_op jit(solution)/shard_map/psum | solution.py:110
  610.0 10.3 %fusion.10 = f32[8,16,64,64]{3,2,1,0:T(8,128)S(1)} fusion(f32[16,70,8,64]{3,2,1,0:T(8,128)} %reshape.2901, f32[8,64,70,1]{2,0,1,3:T(8,128)} %get-tuple-element.61), kind=kOutput, calls=%fused_computation.18 | convolution fusion | flops 440401920 | bytes 4534272 | tf_op jit(solution)/shard_map/txi,yitm->yxtm/dot_general | solution.py:130
  620.4 12.1 %fusion.12 = f32[8,16,64,64]{3,2,1,0:T(8,128)} fusion(f32[16,70,8,64]{3,2,1,0:T(8,128)} %reshape.2900, f32[8,64,70,1]{2,0,1,3:T(8,128)S(1)} %copy-done.17), kind=kOutput, calls=%fused_computation.20 | convolution fusion | flops 440401920 | bytes 4534272 | tf_op jit(solution)/shard_map/txi,yitm->yxtm/dot_general | solution.py:130
  632.5 9.4 %fusion.2 = f32[8,16,64,64]{3,2,1,0:T(8,128)} fusion(f32[16,70,8,64]{3,2,1,0:T(8,128)S(1)} %bitcast.856, f32[8,64,70,1]{2,0,1,3:T(8,128)S(1)} %copy-done.16), kind=kOutput, calls=%fused_computation.10 | convolution fusion | flops 440401920 | bytes 4534272 | tf_op jit(solution)/shard_map/txi,yitm->yxtm/dot_general | solution.py:130
  641.9 9.6 %fusion.4 = f32[8,16,64,64]{3,2,1,0:T(8,128)} fusion(f32[16,70,8,64]{3,2,1,0:T(8,128)S(1)} %bitcast.854, f32[8,64,70,1]{2,0,1,3:T(8,128)S(1)} %copy-done.15), kind=kOutput, calls=%fused_computation.12 | convolution fusion | flops 440401920 | bytes 4534272 | tf_op jit(solution)/shard_map/txi,yitm->yxtm/dot_general | solution.py:130
  651.6 9.5 %fusion.6 = f32[8,16,64,64]{3,2,1,0:T(8,128)} fusion(f32[16,70,8,64]{3,2,1,0:T(8,128)S(1)} %bitcast.852, f32[8,64,70,1]{2,0,1,3:T(8,128)S(1)} %copy-done.14), kind=kOutput, calls=%fused_computation.14 | convolution fusion | flops 440401920 | bytes 4534272 | tf_op jit(solution)/shard_map/txi,yitm->yxtm/dot_general | solution.py:130
  661.1 9.4 %fusion.8 = f32[8,16,64,64]{3,2,1,0:T(8,128)} fusion(f32[16,70,8,64]{3,2,1,0:T(8,128)S(1)} %bitcast.850, f32[8,64,70,1]{2,0,1,3:T(8,128)S(1)} %get-tuple-element.60), kind=kOutput, calls=%fused_computation.16 | convolution fusion | flops 440401920 | bytes 4534272 | tf_op jit(solution)/shard_map/txi,yitm->yxtm/dot_general | solution.py:130
  670.6 13.5 %add_bitcast_fusion = f32[16,64,8,64]{1,3,0,2:T(8,128)} fusion(f32[8,16,64,64]{3,2,1,0:T(8,128)S(1)} %copy-done.10, f32[8,16,64,64]{3,2,1,0:T(8,128)} %fusion.4, f32[8,16,64,64]{3,2,1,0:T(8,128)} %fusion.6, f32[8,16,64,64]{3,2,1,0:T(8,128)} %fusion.8, f32[8,16,64,64]{3,2,1,0:T(8,128)S(1)} %copy-done.9, f32[8,16,64,64]{3,2,1,0:T(8,128)S(1)} %fusion.10, ...), kind=kOutput, calls=%fused_computation.24 | convolution fusion | flops 443547648 | bytes 17117184 | tf_op jit(solution)/shard_map/txi,yitm->yxtm/dot_general | solution.py:130
  689.5 7.8 %convolution_bitcast_fusion = f32[16,64,8,64]{3,2,1,0:T(8,128)} fusion(f32[16,64,8,64]{3,2,1,0:T(8,128)} %copy.99, f32[8,8]{1,0:T(8,128)S(1)} %copy-done.45), kind=kOutput, calls=%fused_computation.40 | convolution fusion | flops 50331648 | bytes 4194560 | tf_op jit(solution)/shard_map/st,yxtm->yxsm/dot_general | solution.py:136
  (322 shorter events, 246.9 us)
Async XLA Ops:
  0.0 562.5 %copy-start = (f32[8,7,7]{2,0,1:T(8,128)S(1)}, f32[8,7,7]{2,0,1:T(8,128)}, u32[]{:S(2)}) copy-start(f32[8,7,7]{2,0,1:T(8,128)} %param.16) | copy-start | bytes 4708
  0.0 24.3 %copy-start.13 = (f32[16,64,512]{2,1,0:T(8,128)S(1)}, f32[16,64,512]{2,1,0:T(8,128)}, u32[]{:S(2)}) copy-start(f32[16,64,512]{2,1,0:T(8,128)} %param.9) | copy-start | bytes 6291460
  29.5 58.3 %copy-start.8 = (f32[1024,8,64]{0,2,1:T(8,128)}, f32[1024,8,64]{0,2,1:T(8,128)S(1)}, u32[]{:S(2)}) copy-start(f32[1024,8,64]{0,2,1:T(8,128)S(1)} %copy.67) | copy-start | bytes 6291460
  93.1 49.6 %copy-start.46 = (f32[8,128]{1,0:T(8,128)S(1)}, f32[8,128]{1,0:T(8,128)}, u32[]{:S(2)}) copy-start(f32[8,128]{1,0:T(8,128)} %param.12) | copy-start | bytes 12292
  96.0 53.6 %copy-start.47 = (f32[8,128]{1,0:T(8,128)S(1)}, f32[8,128]{1,0:T(8,128)}, u32[]{:S(2)}) copy-start(f32[8,128]{1,0:T(8,128)} %param.13) | copy-start | bytes 12292
  96.0 54.2 %copy-start.22 = (f32[16,128]{1,0:T(8,128)S(1)}, f32[16,128]{1,0:T(8,128)}, u32[]{:S(2)}) copy-start(f32[16,128]{1,0:T(8,128)} %get-tuple-element.135) | copy-start | bytes 24580
  157.2 51.1 %copy-start.2 = (f32[1024,8,64]{0,2,1:T(8,128)S(1)}, f32[1024,8,64]{0,2,1:T(8,128)}, u32[]{:S(2)}) copy-start(f32[1024,8,64]{0,2,1:T(8,128)} %fusion.39) | copy-start | bytes 6291460
  161.8 53.9 %copy-start.21 = (f32[16,128]{1,0:T(8,128)S(1)}, f32[16,128]{1,0:T(8,128)}, u32[]{:S(2)}) copy-start(f32[16,128]{1,0:T(8,128)} %get-tuple-element.136) | copy-start | bytes 24580
  222.8 50.8 %copy-start.3 = (f32[1024,8,64]{0,2,1:T(8,128)S(1)}, f32[1024,8,64]{0,2,1:T(8,128)}, u32[]{:S(2)}) copy-start(f32[1024,8,64]{0,2,1:T(8,128)} %fusion.42) | copy-start | bytes 6291460
  227.0 54.1 %copy-start.20 = (f32[16,128]{1,0:T(8,128)S(1)}, f32[16,128]{1,0:T(8,128)}, u32[]{:S(2)}) copy-start(f32[16,128]{1,0:T(8,128)} %get-tuple-element.137) | copy-start | bytes 24580
  288.1 51.1 %copy-start.4 = (f32[1024,8,64]{0,2,1:T(8,128)S(1)}, f32[1024,8,64]{0,2,1:T(8,128)}, u32[]{:S(2)}) copy-start(f32[1024,8,64]{0,2,1:T(8,128)} %fusion.45) | copy-start | bytes 6291460
  292.7 54.0 %copy-start.19 = (f32[16,128]{1,0:T(8,128)S(1)}, f32[16,128]{1,0:T(8,128)}, u32[]{:S(2)}) copy-start(f32[16,128]{1,0:T(8,128)} %get-tuple-element.138) | copy-start | bytes 24580
  353.8 50.8 %copy-start.5 = (f32[1024,8,64]{0,2,1:T(8,128)S(1)}, f32[1024,8,64]{0,2,1:T(8,128)}, u32[]{:S(2)}) copy-start(f32[1024,8,64]{0,2,1:T(8,128)} %fusion.48) | copy-start | bytes 6291460
  358.0 53.9 %copy-start.18 = (f32[16,128]{1,0:T(8,128)S(1)}, f32[16,128]{1,0:T(8,128)}, u32[]{:S(2)}) copy-start(f32[16,128]{1,0:T(8,128)} %get-tuple-element.139) | copy-start | bytes 24580
  419.0 51.1 %copy-start.6 = (f32[1024,8,64]{0,2,1:T(8,128)S(1)}, f32[1024,8,64]{0,2,1:T(8,128)}, u32[]{:S(2)}) copy-start(f32[1024,8,64]{0,2,1:T(8,128)} %fusion.51) | copy-start | bytes 6291460
  550.8 12.5 %collective-permute-start = (f32[3,64,512]{2,1,0:T(8,128)}, f32[3,64,512]{2,1,0:T(8,128)}, u32[]{:S(2)}, u32[]{:S(2)}) collective-permute-start(f32[3,64,512]{2,1,0:T(8,128)} %slice.114), channel_id=1, source_target_pairs={{0,8},{8,16},{16,24},{1,9},{9,17},{17,25},{2,10},{10,18},{18,26},{... | collective-permute-start | bytes 1179656 | tf_op jit(solution)/shard_map/ppermute | solution.py:18
  555.2 9.1 %collective-permute-start.1 = (f32[3,64,512]{2,1,0:T(8,128)S(1)}, f32[3,64,512]{2,1,0:T(8,128)S(1)}, u32[]{:S(2)}, u32[]{:S(2)}) collective-permute-start(f32[3,64,512]{2,1,0:T(8,128)S(1)} %slice.116), channel_id=1, source_target_pairs={{8,0},{16,8},{24,16},{9,1},{17,9},{25,17},{10,2},{18,10},{26,18},{... | collective-permute-start | bytes 1179656 | tf_op jit(solution)/shard_map/ppermute | solution.py:19
  565.2 3.9 collective-permute-start.2
  566.5 6.7 collective-permute-start.3
  607.4 25.0 %slice-start.6 = ((s8[4587520]{0:T(1024)(128)(4,1)}), s8[393216]{0:T(1024)(128)(4,1)S(1)}, s32[]{:S(2)}) async-start(s8[4587520]{0:T(1024)(128)(4,1)} %bitcast.855), calls=%async_computation.6 | async-start | bytes 786432
  610.0 22.4 %slice-start.7 = ((s8[4587520]{0:T(1024)(128)(4,1)}), s8[4194304]{0:T(1024)(128)(4,1)S(1)}, s32[]{:S(2)}) async-start(s8[4587520]{0:T(1024)(128)(4,1)} %bitcast.855), calls=%async_computation.7 | async-start | bytes 8388608
  620.4 21.5 %slice-start.4 = ((s8[4587520]{0:T(1024)(128)(4,1)}), s8[4194304]{0:T(1024)(128)(4,1)S(1)}, s32[]{:S(2)}) async-start(s8[4587520]{0:T(1024)(128)(4,1)} %bitcast.853), calls=%async_computation.4 | async-start | bytes 8388608
  620.4 31.2 %slice-start.2 = ((s8[4587520]{0:T(1024)(128)(4,1)}), s8[4194304]{0:T(1024)(128)(4,1)S(1)}, s32[]{:S(2)}) async-start(s8[4587520]{0:T(1024)(128)(4,1)} %bitcast.851), calls=%async_computation.2 | async-start | bytes 8388608
  641.9 19.2 %slice-start = ((s8[4587520]{0:T(1024)(128)(4,1)}), s8[4194304]{0:T(1024)(128)(4,1)S(1)}, s32[]{:S(2)}) async-start(s8[4587520]{0:T(1024)(128)(4,1)} %bitcast.849), calls=%async_computation | async-start | bytes 8388608
  (52 other events, 354.4 us)
